TPU v7x, 256 devices: a whole 4x4x8 slice. The times are simulated.
256 devices in a mesh: group: 16 (over z, core), dev: 16 (over y, x).
Axes of the slice: x: 4, y: 4, z: 8, core: 2. Of those that a mesh axis runs over, the one named last changes fastest.
Arguments:
- tokens: bfloat16 [1024, 7168], P(('group', 'dev')), may hold values from -6 to 6
- group_ids: int32 [1024, 4], P(('group', 'dev')), may hold values from 0 to 15, as said below
- expert_ids: int32 [1024, 8], P(('group', 'dev')), may hold values from 0 to 63, as said below
- gate_scores: bfloat16 [1024, 8], P(('group', 'dev')), may hold values from 0.099609375 to 1
- w_gate: bfloat16 [7168, 65536], P(None, ('group', 'dev')), may hold values from -0.0625 to 0.0625
- w_up: bfloat16 [7168, 65536], P(None, ('group', 'dev')), may hold values from -0.0625 to 0.0625
- w_down: bfloat16 [65536, 7168], P(('group', 'dev')), may hold values from -0.1875 to 0.1875
Outputs:
- combined: bfloat16 [1024, 7168], P(('group', 'dev'))
Inputs may be any that keep to these rules, and one draw needn't show every extreme that they name: `group_ids`: each row names 4 different groups; among the 4 rows of one aligned block, at most 2 rows name any one group. `expert_ids`: each row names 8 different experts, exactly two in each group of the row's group_ids (expert x lies in group x // 4).
All inputs are finite; a program needn't handle non-finite values.
Results may differ from a plain program's by a relative error of at most 0.014.
Values may be sent and summed in bfloat16 or wider, within the bound.
No kernel may reach another device: no remote copies, remote signals or barrier semaphores. Data moves between devices by JAX's collectives and lax.ppermute only.
A program may use at most 64 MiB of HBM per device.

v0:
```python
import jax
import jax.numpy as jnp
from jax import lax
from jax.sharding import PartitionSpec as P

FF = 1024
EXP_GROUP = 4
CAP = 2


def local(tokens, group_ids, expert_ids, gate_scores, w_gate, w_up, w_down):
    group_count = lax.axis_size("group")
    dev_count = lax.axis_size("dev")
    model_width = tokens.shape[1]
    block_cols = w_gate.shape[1]
    expert_total = group_count * EXP_GROUP
    group_iota = jnp.arange(group_count, dtype=jnp.int32)
    member = jnp.sum((group_ids[:, :, None] == group_iota[None, None, :]).astype(jnp.int32), axis=1)
    before = jnp.cumsum(member, axis=0) - member
    slot_iota = jnp.arange(CAP, dtype=jnp.int32)
    select = (member.T[:, None, :] == 1) & (before.T[:, None, :] == slot_iota[None, :, None])
    select_rows = select.astype(jnp.bfloat16)
    matches = (
        expert_ids[:, :, None] == jnp.arange(expert_total, dtype=jnp.int32)[None, None, :]
    ).astype(jnp.float32)
    coef = jnp.sum(gate_scores.astype(jnp.float32)[:, :, None] * matches, axis=1)
    coef = coef.reshape(-1, group_count, EXP_GROUP).astype(jnp.bfloat16)
    send_rows = jnp.einsum(
        "gst,td->gsd", select_rows, tokens, preferred_element_type=jnp.float32
    ).astype(jnp.bfloat16)
    send_coef = jnp.einsum(
        "gst,tge->gse", select_rows, coef, preferred_element_type=jnp.float32
    ).astype(jnp.bfloat16)
    recv_rows, recv_coef = (
        lax.all_to_all(send_rows, "group", split_axis=0, concat_axis=0, tiled=True),
        lax.all_to_all(send_coef, "group", split_axis=0, concat_axis=0, tiled=True),
    )
    all_rows, all_coef = (
        lax.all_gather(recv_rows, "dev", axis=0, tiled=True),
        lax.all_gather(recv_coef, "dev", axis=0, tiled=True),
    )
    flat_rows = all_rows.reshape(-1, model_width)
    flat_coef = all_coef.reshape(-1, EXP_GROUP)
    dev_index = lax.axis_index("dev")
    owner_expert = (dev_index * block_cols + jnp.arange(block_cols, dtype=jnp.int32)) // FF
    onehot = (owner_expert[None, :] == jnp.arange(EXP_GROUP, dtype=jnp.int32)[:, None]).astype(
        jnp.bfloat16
    )
    gate_out = jnp.dot(flat_rows, w_gate, preferred_element_type=jnp.float32)
    up_out = jnp.dot(flat_rows, w_up, preferred_element_type=jnp.float32)
    col_scale = jnp.dot(flat_coef, onehot, preferred_element_type=jnp.float32)
    hidden = (col_scale * jax.nn.silu(gate_out) * up_out).astype(jnp.bfloat16)
    partial_value = lax.optimization_barrier(
        jnp.dot(hidden, w_down, preferred_element_type=jnp.float32).astype(jnp.bfloat16)
    )
    partial_value = partial_value.reshape(dev_count, group_count, CAP, model_width)
    moved_back = lax.all_to_all(partial_value, "group", split_axis=1, concat_axis=1, tiled=True)
    summed = lax.psum_scatter(
        moved_back.astype(jnp.float32).astype(jnp.bfloat16), "dev", scatter_dimension=0, tiled=True
    )
    returned = summed.reshape(group_count, CAP, model_width)
    combined = jnp.einsum("gst,gsd->td", select_rows, returned, preferred_element_type=jnp.float32)
    return combined.astype(jnp.bfloat16)


def solution(mesh):
    return jax.shard_map(
        local,
        mesh=mesh,
        in_specs=(
            P(("group", "dev"), None),
            P(("group", "dev"), None),
            P(("group", "dev"), None),
            P(("group", "dev"), None),
            P(None, ("group", "dev")),
            P(None, ("group", "dev")),
            P(("group", "dev"), None),
        ),
        out_specs=P(("group", "dev"), None),
        check_vma=False,
    )
```

profile of v0, /device:TPU:2, one launch (start us, length us, event | category | flops | bytes accessed | tf_op | source)
XLA Modules:
  0.0 424.0 jit_solution(7251178532512982187)
XLA Ops:
  6.5 0.8 convert_reduce_fusion
  7.4 0.4 convolution_convert_fusion.1
  7.8 0.5 copy.26
  8.2 23.2 %all_to_all.15 = bf16[16,2,7168]{2,1,0:T(2,128)(2,1)} all-to-all(bf16[16,2,7168]{2,1,0:T(2,128)(2,1)S(1)} %copy.26), channel_id=1, replica_groups=mesh['group'=16,'dev'=16] {'group'}, dimensions={0} | all-to-all | bytes 917504 | tf_op jit(solution)/shard_map/all_to_all | solution.py:35
  31.5 0.1 copy.24
  31.6 0.7 convert_element_type.33
  32.3 0.8 select_reduce_fusion
  33.1 0.1 convert_element_type.35
  33.2 0.8 convolution_convert_fusion.2
  33.9 4.0 all-to-all-start
  38.0 7.5 %all-to-all-done = bf16[16,2,4]{2,1,0:T(2,128)(2,1)S(1)} async-done(((bf16[16,2,4]{2,1,0:T(2,128)(2,1)}), bf16[16,2,4]{2,1,0:T(2,128)(2,1)S(1)}, u32[]{:S(2)}, u32[]{:S(2)}) %all-to-all-start) | async-done | bytes 288 | tf_op jit(solution)/shard_map/all_to_all | solution.py:36
  45.5 23.8 %all_gather.6 = bf16[256,2,4]{2,1,0:T(2,128)(2,1)S(1)} all-gather(bf16[16,2,4]{2,1,0:T(2,128)(2,1)S(1)} %all-to-all-done), channel_id=1, replica_groups=mesh['group'=16,'dev'=16] {'dev'}, dimensions={0}, use_global_device_ids=true | all-gather | bytes 4352 | tf_op jit(solution)/shard_map/all_gather | solution.py:40
  69.3 32.0 %all-gather.2.cloned.1.call-done = bf16[256,2,7168]{2,1,0:T(2,128)(2,1)} async-done(((bf16[16,2,7168]{2,1,0:T(2,128)(2,1)}), bf16[256,2,7168]{2,1,0:T(2,128)(2,1)}) %all-gather.2.cloned.1.call-update) | async-done | bytes 7340048 | tf_op jit(solution)/shard_map/all_gather | solution.py:39
  101.3 15.4 %reshape.40 = bf16[512,7168]{1,0:T(8,128)(2,1)} reshape(bf16[256,2,7168]{2,1,0:T(2,128)(2,1)} %all-gather.2.cloned.1.call-done) | data formatting | bytes 14680064 | tf_op jit(solution)/shard_map/reshape | solution.py:42
  116.7 6.3 %fusion.16 = f32[512,256]{1,0:T(8,128)S(1)} fusion(bf16[512,7168]{1,0:T(8,128)(2,1)} %reshape.40, bf16[7168,256]{1,0:T(8,128)(2,1)} %param.11), kind=kOutput, calls=%fused_computation.32 | convolution fusion | flops 1879048192 | bytes 11534336 | tf_op jit(solution)/shard_map/dot_general | solution.py:49
  123.1 0.9 copy-done.2
  124.0 2.1 fusion.17
  126.0 6.4 %convolution_convert_fusion = bf16[512,7168]{1,0:T(8,128)(2,1)} fusion(bf16[256,7168]{1,0:T(8,128)(2,1)} %param.13, f32[512,256]{1,0:T(8,128)S(1)} %fusion.17, bf16[512,4]{1,0:T(8,128)(2,1)S(1)} %bitcast.25, f32[512,256]{1,0:T(8,128)S(1)} %fusion.16, s32[256]{0:T(256)S(1)} %and_select_fusion), kind=kOutput, calls=%fused_computation | convolution fusion | flops 1884685312 | bytes 12063744 | tf_op jit(solution)/shard_map/dot_general | solution.py:54
  132.4 14.9 %reshape.41 = bf16[16,16,2,7168]{3,2,1,0:T(2,128)(2,1)} reshape(bf16[512,7168]{1,0:T(8,128)(2,1)} %convolution_convert_fusion) | data formatting | bytes 14680064 | tf_op jit(solution)/shard_map/reshape | solution.py:56
  147.3 6.6 %copy.27 = bf16[16,16,2,7168]{3,2,0,1:T(2,128)(2,1)S(1)} copy(bf16[16,16,2,7168]{3,2,1,0:T(2,128)(2,1)} %reshape.41) | data formatting | bytes 14680064 | tf_op jit(solution)/shard_map/reshape | solution.py:56
  153.9 168.9 %all_to_all.16 = bf16[16,16,2,7168]{3,2,0,1:T(2,128)(2,1)S(1)} all-to-all(bf16[16,16,2,7168]{3,2,0,1:T(2,128)(2,1)S(1)} %copy.27), channel_id=1, replica_groups=mesh['group'=16,'dev'=16] {'group'}, dimensions={1} | all-to-all | bytes 14680064 | tf_op jit(solution)/shard_map/all_to_all | solution.py:57
  322.8 7.0 %copy.28 = bf16[16,16,2,7168]{3,1,2,0:T(8,128)(2,1)} copy(bf16[16,16,2,7168]{3,2,0,1:T(2,128)(2,1)S(1)} %all_to_all.16) | data formatting | bytes 14680064 | tf_op jit(solution)/shard_map/all_to_all | solution.py:57
  329.8 85.4 %reduce-scatter.4.cloned.1.call-done = bf16[1,16,2,7168]{3,1,2,0:T(8,128)(2,1)} async-done(((bf16[16,16,2,7168]{3,1,2,0:T(8,128)(2,1)}), bf16[1,16,2,7168]{3,1,2,0:T(8,128)(2,1)}) %reduce-scatter.4.cloned.1.call-update) | async-done | bytes 458768
  415.2 1.9 fusion
  (14 shorter events, 0.2 us)
Async XLA Ops:
  6.5 0.9 copy-start
  6.5 94.7 %all-gather.2.cloned.1.call-start = ((), (), s32[]{:S(2)}) async-start(), calls=%async_computation.4 | async-start | bytes 7798784 | tf_op jit(solution)/shard_map/all_gather | solution.py:39
  33.9 11.5 %all-to-all-start = ((bf16[16,2,4]{2,1,0:T(2,128)(2,1)}), bf16[16,2,4]{2,1,0:T(2,128)(2,1)S(1)}, u32[]{:S(2)}, u32[]{:S(2)}) async-start(bf16[16,2,4]{2,1,0:T(2,128)(2,1)} %convolution_convert_fusion.2), calls=%async_computation | async-start | bytes 16384 | tf_op jit(solution)/shard_map/all_to_all | solution.py:36
  38.0 377.3 %reduce-scatter.4.cloned.1.call-start = ((), (), s32[]{:S(2)}) async-start(), calls=%async_computation.5 | async-start | bytes 7798784
  116.7 6.3 %copy-start.1 = (bf16[512,7168]{1,0:T(8,128)(2,1)S(1)}, bf16[512,7168]{1,0:T(8,128)(2,1)}, u32[]{:S(2)}) copy-start(bf16[512,7168]{1,0:T(8,128)(2,1)} %reshape.40) | copy-start | bytes 22020100
  116.7 7.3 %copy-start.2 = (bf16[7168,256]{1,0:T(8,128)(2,1)S(1)}, bf16[7168,256]{1,0:T(8,128)(2,1)}, u32[]{:S(2)}) copy-start(bf16[7168,256]{1,0:T(8,128)(2,1)} %param.12) | copy-start | bytes 11010052
Sparse Core Ops, SparseCore 0:
  31.6 69.5 all-gather.1
  330.0 85.2 reduce-scatter.3
where the time goes:
time: 425 us; the launch traced here: 424 us
  blocking collectives  216 us (51%)
  waiting for transfers between devices  125 us (29%)
  local copies, waits for them, and re-layouts  45.5 us (11%)
  matrix products  17.8 us (4%)
  between operations  13.5 us (3%)
    all_to_all x1, blocking collectives, local(): lax.all_to_all(partial_value, 'group', split_axis=1, concat_axis=1, tiled...  169 us
    unnamed x3, waiting for transfers between devices  85.4 us
    all_gather x1, waiting for transfers between devices, local(): lax.all_gather(recv_rows, 'dev', axis=0, tiled=True)  32 us
    all_gather x1, blocking collectives, local(): lax.all_gather(recv_coef, 'dev', axis=0, tiled=True)  23.8 us
    all_to_all x1, blocking collectives, local(): lax.all_to_all(send_rows, 'group', split_axis=0, concat_axis=0, tiled=True)  23.2 us
    reshape x2, local copies, waits for them, and re-layouts, local(): partial_value.reshape(dev_count, group_count, CAP, model_width)  21.5 us
    reshape x1, local copies, waits for them, and re-layouts, local(): flat_rows = all_rows.reshape(-1, model_width)  15.4 us
  transfers between devices with their start and end apart: 3, of which 3 were waited for; matrix products, arithmetic and copies ran while one was open for 1% of the time, Pallas kernels for 0%

commit v1 on v0

--- a/solution.py
+++ b/solution.py
@@ -54,7 +54,12 @@
         jnp.dot(hidden, w_down, preferred_element_type=jnp.float32).astype(jnp.bfloat16)
     )
     partial_value = partial_value.reshape(dev_count, group_count, CAP, model_width)
-    moved_back = lax.all_to_all(partial_value, "group", split_axis=1, concat_axis=1, tiled=True)
+    moved_back = jnp.concatenate(
+        lax.all_to_all(
+            jnp.stack(jnp.split(partial_value, lax.axis_size("group"), axis=1)), "group", 0, 0
+        ),
+        axis=1,
+    )
     summed = lax.psum_scatter(
         moved_back.astype(jnp.float32).astype(jnp.bfloat16), "dev", scatter_dimension=0, tiled=True
     )

time: 425 us -> 430 us (1.012)
  local copies, waits for them, and re-layouts: 45.5 us -> 50.6 us
    split x0 -> x1, local copies, waits for them, and re-layouts: none -> 10.5 us  [local(): jnp.split(partial_value, lax.axis_size('group'), axis=1)]
    all_to_all x1 -> x0, local copies, waits for them, and re-layouts: 6.98 us -> none  [local(): lax.all_to_all(partial_value, 'group', split_axis=1, concat_axis=1, tiled...]
    reshape x0 -> x1, local copies, waits for them, and re-layouts: none -> 6.97 us  [local(): jnp.concatenate(lax.all_to_all(jnp.stack(jnp.split(partial_value, lax.axi...]
    reshape x2 -> x1, local copies, waits for them, and re-layouts: 21.5 us -> 14.9 us  [local(): partial_value.reshape(dev_count, group_count, CAP, model_width)]
where the time goes in v1:
time: 430 us; the launch traced here: 429 us
  blocking collectives  216 us (50%)
  waiting for transfers between devices  125 us (29%)
  local copies, waits for them, and re-layouts  50.6 us (12%)
  matrix products  17.8 us (4%)
  between operations  13.6 us (3%)
    all_to_all x1, blocking collectives, local(): lax.all_to_all(jnp.stack(jnp.split(partial_value, lax.axis_size('group'),...  169 us
    unnamed x3, waiting for transfers between devices  85.4 us
    all_gather x1, waiting for transfers between devices, local(): lax.all_gather(recv_rows, 'dev', axis=0, tiled=True)  32 us
    all_gather x1, blocking collectives, local(): lax.all_gather(recv_coef, 'dev', axis=0, tiled=True)  23.8 us
    all_to_all x1, blocking collectives, local(): lax.all_to_all(send_rows, 'group', split_axis=0, concat_axis=0, tiled=True)  23.2 us
    reshape x1, local copies, waits for them, and re-layouts, local(): flat_rows = all_rows.reshape(-1, model_width)  15.4 us
    reshape x1, local copies, waits for them, and re-layouts, local(): partial_value.reshape(dev_count, group_count, CAP, model_width)  14.9 us
    split x1, local copies, waits for them, and re-layouts, local(): jnp.split(partial_value, lax.axis_size('group'), axis=1)  10.5 us
  transfers between devices with their start and end apart: 3, of which 3 were waited for; matrix products, arithmetic and copies ran while one was open for 1% of the time, Pallas kernels for 0%

profile of v1, /device:TPU:2, one launch (start us, length us, event | category | flops | bytes accessed | tf_op | source)
XLA Modules:
  0.0 429.2 jit_solution(11863718024750651615)
XLA Ops:
  6.5 0.8 convert_reduce_fusion
  7.4 0.4 convolution_convert_fusion.1
  7.8 0.5 copy.107
  8.2 23.2 %all_to_all.15 = bf16[16,2,7168]{2,1,0:T(2,128)(2,1)} all-to-all(bf16[16,2,7168]{2,1,0:T(2,128)(2,1)S(1)} %copy.107), channel_id=1, replica_groups=mesh['group'=16,'dev'=16] {'group'}, dimensions={0} | all-to-all | bytes 917504 | tf_op jit(solution)/shard_map/all_to_all | solution.py:35
  31.5 0.1 copy.105
  31.6 0.7 convert_element_type.33
  32.3 0.8 select_reduce_fusion
  33.1 0.1 convert_element_type.35
  33.2 0.8 convolution_convert_fusion.2
  33.9 4.0 all-to-all-start
  38.0 7.5 %all-to-all-done = bf16[16,2,4]{2,1,0:T(2,128)(2,1)S(1)} async-done(((bf16[16,2,4]{2,1,0:T(2,128)(2,1)}), bf16[16,2,4]{2,1,0:T(2,128)(2,1)S(1)}, u32[]{:S(2)}, u32[]{:S(2)}) %all-to-all-start) | async-done | bytes 288 | tf_op jit(solution)/shard_map/all_to_all | solution.py:36
  45.5 23.8 %all_gather.6 = bf16[256,2,4]{2,1,0:T(2,128)(2,1)S(1)} all-gather(bf16[16,2,4]{2,1,0:T(2,128)(2,1)S(1)} %all-to-all-done), channel_id=1, replica_groups=mesh['group'=16,'dev'=16] {'dev'}, dimensions={0}, use_global_device_ids=true | all-gather | bytes 4352 | tf_op jit(solution)/shard_map/all_gather | solution.py:40
  69.3 32.0 %all-gather.2.cloned.1.call-done = bf16[256,2,7168]{2,1,0:T(2,128)(2,1)} async-done(((bf16[16,2,7168]{2,1,0:T(2,128)(2,1)}), bf16[256,2,7168]{2,1,0:T(2,128)(2,1)}) %all-gather.2.cloned.1.call-update) | async-done | bytes 7340048 | tf_op jit(solution)/shard_map/all_gather | solution.py:39
  101.3 15.4 %reshape.46 = bf16[512,7168]{1,0:T(8,128)(2,1)} reshape(bf16[256,2,7168]{2,1,0:T(2,128)(2,1)} %all-gather.2.cloned.1.call-done) | data formatting | bytes 14680064 | tf_op jit(solution)/shard_map/reshape | solution.py:42
  116.7 6.3 %fusion.34 = f32[512,256]{1,0:T(8,128)S(1)} fusion(bf16[512,7168]{1,0:T(8,128)(2,1)} %reshape.46, bf16[7168,256]{1,0:T(8,128)(2,1)} %param.12), kind=kOutput, calls=%fused_computation.66 | convolution fusion | flops 1879048192 | bytes 11534336 | tf_op jit(solution)/shard_map/dot_general | solution.py:50
  123.1 0.9 copy-done.3
  124.0 2.1 fusion.33
  126.0 6.4 %convolution_convert_fusion = bf16[512,7168]{1,0:T(8,128)(2,1)} fusion(bf16[256,7168]{1,0:T(8,128)(2,1)} %param.13, f32[512,256]{1,0:T(8,128)S(1)} %fusion.34, bf16[512,4]{1,0:T(8,128)(2,1)S(1)} %bitcast.93, f32[512,256]{1,0:T(8,128)S(1)} %fusion.33, s32[256]{0:T(256)S(1)} %and_select_fusion), kind=kOutput, calls=%fused_computation | convolution fusion | flops 1884685312 | bytes 12063744 | tf_op jit(solution)/shard_map/dot_general | solution.py:54
  132.4 14.9 %reshape.47 = bf16[16,16,2,7168]{3,2,1,0:T(2,128)(2,1)} reshape(bf16[512,7168]{1,0:T(8,128)(2,1)} %convolution_convert_fusion) | data formatting | bytes 14680064 | tf_op jit(solution)/shard_map/reshape | solution.py:56
  147.3 10.5 %fusion.32 = (bf16[16,1,2,7168]{3,2,1,0:T(2,128)(2,1)S(1)}, bf16[16,1,2,7168]{3,2,1,0:T(2,128)(2,1)S(1)}, bf16[16,1,2,7168]{3,2,1,0:T(2,128)(2,1)S(1)}, bf16[16,...) fusion(bf16[16,16,2,7168]{3,2,1,0:T(2,128)(2,1)} %reshape.47), kind=kLoop, calls=%fused_computation.64 | loop fusion | bytes 14680064 | tf_op jit(solution)/shard_map/split | solution.py:59
  159.1 168.9 %all_to_all.16 = bf16[16,16,1,2,7168]{4,1,3,2,0:T(8,128)(2,1)S(1)} all-to-all(bf16[16,16,1,2,7168]{4,1,3,2,0:T(8,128)(2,1)S(1)} %fusion.8), channel_id=1, replica_groups=mesh['group'=16,'dev'=16] {'group'}, dimensions={0} | all-to-all | bytes 14680064 | tf_op jit(solution)/shard_map/all_to_all | solution.py:58
  328.1 7.0 %copy.124 = bf16[16,16,2,7168]{3,1,2,0:T(8,128)(2,1)} copy(bf16[16,16,2,7168]{3,0,2,1:T(8,128)(2,1)S(1)} %bitcast.92) | data formatting | bytes 14680064 | tf_op jit(solution)/shard_map/reshape | solution.py:57
  335.1 85.4 %reduce-scatter.4.cloned.1.call-done = bf16[1,16,2,7168]{3,1,2,0:T(8,128)(2,1)} async-done(((bf16[16,16,2,7168]{3,1,2,0:T(8,128)(2,1)}), bf16[1,16,2,7168]{3,1,2,0:T(8,128)(2,1)}) %reduce-scatter.4.cloned.1.call-update) | async-done | bytes 458768
  420.5 1.9 fusion
  (32 shorter events, 1.4 us)
Async XLA Ops:
  6.5 0.9 copy-start
  6.5 94.7 %all-gather.2.cloned.1.call-start = ((), (), s32[]{:S(2)}) async-start(), calls=%async_computation.4 | async-start | bytes 7798784 | tf_op jit(solution)/shard_map/all_gather | solution.py:39
  33.9 11.5 %all-to-all-start = ((bf16[16,2,4]{2,1,0:T(2,128)(2,1)}), bf16[16,2,4]{2,1,0:T(2,128)(2,1)S(1)}, u32[]{:S(2)}, u32[]{:S(2)}) async-start(bf16[16,2,4]{2,1,0:T(2,128)(2,1)} %convolution_convert_fusion.2), calls=%async_computation | async-start | bytes 16384 | tf_op jit(solution)/shard_map/all_to_all | solution.py:36
  38.0 382.5 %reduce-scatter.4.cloned.1.call-start = ((), (), s32[]{:S(2)}) async-start(), calls=%async_computation.5 | async-start | bytes 7798784
  116.7 6.3 %copy-start.2 = (bf16[512,7168]{1,0:T(8,128)(2,1)S(1)}, bf16[512,7168]{1,0:T(8,128)(2,1)}, u32[]{:S(2)}) copy-start(bf16[512,7168]{1,0:T(8,128)(2,1)} %reshape.46) | copy-start | bytes 22020100
  116.7 7.3 %copy-start.3 = (bf16[7168,256]{1,0:T(8,128)(2,1)S(1)}, bf16[7168,256]{1,0:T(8,128)(2,1)}, u32[]{:S(2)}) copy-start(bf16[7168,256]{1,0:T(8,128)(2,1)} %param.11) | copy-start | bytes 11010052
  328.1 94.3 %copy-start.1 = (bf16[4,7168]{1,0:T(4,128)(2,1)S(1)}, bf16[4,7168]{1,0:T(4,128)(2,1)}, u32[]{:S(2)}) copy-start(bf16[4,7168]{1,0:T(4,128)(2,1)} %param.7) | copy-start | bytes 172036
Sparse Core Ops, SparseCore 0:
  31.6 69.5 all-gather.1
  335.2 85.2 reduce-scatter.3
